TPU v7x, 128 devices: a whole 4x4x4 slice. The times are simulated.
128 devices in a mesh: row: 16 (over y, x), col: 8 (over z, core).
Axes of the slice: x: 4, y: 4, z: 4, core: 2. Of those that a mesh axis runs over, the one named last changes fastest.
Arguments:
- tokens: bfloat16 [16384, 1280], P(('row', 'col')), may hold values from -6 to 6
- image_sizes: int32 [16, 8], replicated, may hold values from 1 to 48, 256 in all within a row
- slot_of: int32 [128], replicated, may hold values from 0 to 127, as said below
- ln_gain: float32 [1, 2, 1280], replicated, may hold values from 0.25 to 1.75
- ln_bias: float32 [1, 2, 1280], replicated, may hold values from -3 to 3
- w_qkv: bfloat16 [1, 1280, 3840], P(None, 'row', 'col')
- w_out: bfloat16 [1, 1280, 1280], P(None, 'col', 'row'), may hold values from -0.15625 to 0.15625
- w_up: bfloat16 [1, 1280, 5120], P(None, 'row', 'col'), may hold values from -0.15625 to 0.15625
- w_down: bfloat16 [1, 5120, 1280], P(None, 'col', 'row'), may hold values from -0.078125 to 0.078125
- merge_gain: float32 [1280], replicated, may hold values from 0.25 to 1.75
- merge_bias: float32 [1280], replicated, may hold values from -3 to 3
- w_merge: bfloat16 [5120, 4096], P('row', 'col'), may hold values from -0.078125 to 0.078125
Outputs:
- merged_out: bfloat16 [6144, 4096], P('row', 'col')
- req_norm: float32 [128], P('row')
- req_max: float32 [128], P('row')
Inputs may be any that keep to these rules, and one draw needn't show every extreme that they name: Each row of image_sizes sums to 256 and holds 48 at least once. A permutation of the slots. Request g * 8 + j goes to the row group slot_of // 8, which holds 8 slots. No row group sends more than one request to any row group.
All inputs are finite; a program needn't handle non-finite values.
Results may differ from a plain program's by a relative error of at most 0.018.
The roundings to bfloat16 on the way count: a program that leaves them out, or rounds other values in their place, can miss the bound.
Values may be sent and summed in bfloat16 or wider, within the bound.
A program may use at most 64 MiB of HBM per device.

v0:
```python
import jax
import jax.numpy as jnp
from jax import lax
from jax.sharding import PartitionSpec as P

D = 1280
HEAD_DIM = 80
OUT = 4096
IMG_ROW = 8


def layer_norm(values, gain, bias):
    center = jnp.mean(values, axis=-1, keepdims=True)
    shifted = values - center
    spread = jnp.mean(shifted * shifted, axis=-1, keepdims=True)
    return shifted * lax.rsqrt(spread + 1e-06) * gain + bias


def segment_ids(sizes_row, count):
    bounds = jnp.cumsum(sizes_row)
    merged_index = jnp.arange(count, dtype=jnp.int32) // 4
    return jnp.sum((merged_index[:, None] >= bounds[None, :]).astype(jnp.int32), axis=1)


def attend(qkv, segments):
    count = qkv.shape[0]
    width = min(512, count)
    query = qkv[:, :, 0]
    keys = qkv[:, :, 1]
    values = qkv[:, :, 2]
    results = []
    for offset in range(0, count, width):
        scores = jnp.einsum(
            "qhd,khd->hqk", query[offset : offset + width], keys, preferred_element_type=jnp.float32
        ) * HEAD_DIM ** (-0.5)
        same = segments[offset : offset + width, None] == segments[None, :]
        scores = jnp.where(same[None], scores, -1e30)
        peak = jnp.max(scores, axis=-1, keepdims=True)
        expo = jnp.exp(scores - peak)
        weights = (expo / jnp.sum(expo, axis=-1, keepdims=True)).astype(jnp.bfloat16)
        context = jnp.einsum("hqk,khd->qhd", weights, values, preferred_element_type=jnp.float32)
        results.append(context.astype(jnp.bfloat16).reshape(width, -1))
    return jnp.concatenate(results, axis=0)


def local(
    tokens,
    image_sizes,
    slot_of,
    ln_gain,
    ln_bias,
    w_qkv,
    w_out,
    w_up,
    w_down,
    merge_gain,
    merge_bias,
    w_merge,
):
    n_col = lax.axis_size("col")
    row_index = lax.axis_index("row")
    tok_dev = tokens.shape[0]
    tok_row = tok_dev * n_col
    merged_row = tok_row // 4
    most = merged_row * 3 // 16
    sizes_here = lax.dynamic_index_in_dim(image_sizes, row_index, 0, keepdims=False)
    segments = segment_ids(sizes_here, tok_row)
    stream = tokens
    normed = layer_norm(stream.astype(jnp.float32), ln_gain[0, 0], ln_bias[0, 0]).astype(
        jnp.bfloat16
    )
    normed_all = lax.all_gather(normed, "col", axis=0, tiled=True)
    left_part = normed_all
    qkv = jnp.dot(
        left_part,
        lax.all_gather(w_qkv[0], "row", axis=0, tiled=True),
        preferred_element_type=jnp.float32,
    )
    qkv = qkv.astype(jnp.bfloat16).reshape(tok_row, -1, 3, HEAD_DIM)
    context = attend(qkv, segments)
    attn_terms = jnp.dot(
        context,
        lax.all_gather(w_out[0], "row", axis=1, tiled=True),
        preferred_element_type=jnp.float32,
    )
    attn_out = lax.psum_scatter(
        attn_terms.astype(jnp.bfloat16), "col", scatter_dimension=0, tiled=True
    ).astype(jnp.float32)
    stream = (stream.astype(jnp.float32) + attn_out).astype(jnp.bfloat16)
    normed = layer_norm(stream.astype(jnp.float32), ln_gain[0, 1], ln_bias[0, 1]).astype(
        jnp.bfloat16
    )
    normed_mlp = lax.all_gather(normed, "col", axis=0, tiled=True)
    left_part = normed_mlp
    up_value = jnp.dot(
        left_part,
        lax.all_gather(w_up[0], "row", axis=0, tiled=True),
        preferred_element_type=jnp.float32,
    )
    hidden = jax.nn.gelu(up_value, approximate=False).astype(jnp.bfloat16)
    mlp_terms = jnp.dot(
        hidden,
        lax.all_gather(w_down[0], "row", axis=1, tiled=True),
        preferred_element_type=jnp.float32,
    )
    mlp_out = lax.psum_scatter(
        mlp_terms.astype(jnp.bfloat16), "col", scatter_dimension=0, tiled=True
    ).astype(jnp.float32)
    stream = (stream.astype(jnp.float32) + mlp_out).astype(jnp.bfloat16)
    merged = layer_norm(stream.astype(jnp.float32), merge_gain, merge_bias).astype(jnp.bfloat16)
    merged = merged.reshape(tok_dev // 4, 4 * D)
    merged_all = lax.all_gather(merged, "col", axis=0, tiled=True)
    out_dev = w_merge.shape[1]
    left_part = merged_all
    projected = jnp.dot(
        left_part,
        lax.all_gather(w_merge, "row", axis=0, tiled=True),
        preferred_element_type=jnp.float32,
    ).astype(jnp.bfloat16)
    reqs = slot_of.shape[0]
    numbers = jnp.arange(reqs, dtype=jnp.int32)
    req_at_slot = jnp.sum(
        jnp.where(slot_of[None, :] == numbers[:, None], numbers[None, :], 0), axis=1
    )
    starts = jnp.cumsum(image_sizes, axis=1) - image_sizes
    starts_flat = starts.reshape(-1)
    sizes_flat = image_sizes.reshape(-1)
    inner = jnp.arange(most, dtype=jnp.int32)
    request = lax.dynamic_slice_in_dim(req_at_slot, row_index * IMG_ROW, IMG_ROW)
    group = request // IMG_ROW
    source = ((group * merged_row + starts_flat[request])[:, None] + inner[None, :]).reshape(-1)
    valid = (inner[None, :] < sizes_flat[request][:, None]).reshape(-1)
    rows_init = jnp.zeros((IMG_ROW * most, out_dev), jnp.bfloat16)
    piece = lax.all_gather(projected, "row", axis=0, tiled=True)
    inside = valid & (source >= 0) & (source < piece.shape[0])
    taken = jnp.take(piece, jnp.clip(source, 0, piece.shape[0] - 1), axis=0)
    placed = jnp.where(inside[:, None], taken, rows_init)
    blocks = placed.astype(jnp.float32).reshape(IMG_ROW, most, out_dev)
    squares = jnp.sum(blocks * blocks, axis=(1, 2))
    peaks = jnp.max(jnp.abs(blocks), axis=(1, 2))
    squares = lax.psum(squares, "col")
    peaks = lax.pmax(peaks, "col")
    slot_size = sizes_flat[request].astype(jnp.float32)
    req_norm = jnp.sqrt(squares / (slot_size * OUT) + 1e-06)
    merged_out = (
        (blocks / req_norm[:, None, None]).astype(jnp.bfloat16).reshape(IMG_ROW * most, out_dev)
    )
    return (merged_out, req_norm, peaks)


def solution(mesh):
    in_specs = (
        P(("row", "col"), None),
        P(),
        P(),
        P(),
        P(),
        P(None, "row", "col"),
        P(None, "col", "row"),
        P(None, "row", "col"),
        P(None, "col", "row"),
        P(),
        P(),
        P("row", "col"),
    )
    out_specs = (P("row", "col"), P("row"), P("row"))
    return jax.shard_map(local, mesh=mesh, in_specs=in_specs, out_specs=out_specs, check_vma=False)
```

profile of v0, /device:TPU:1, one launch (start us, length us, event | category | flops | bytes accessed | tf_op | source)
XLA Modules:
  0.0 487.1 jit_solution(6885048592995645499)
XLA Ops:
  9.9 1.2 fusion.45
  11.1 2.0 fusion.48
  15.1 22.5 %all-gather.1 = bf16[1,160,1280]{1,0,2:T(2,128)(2,1)S(1)} all-gather(bf16[1,160,80]{1,0,2:T(2,128)(2,1)S(1)} %copy.48), channel_id=3, replica_groups=mesh['row'=16,'col'=8] {'row'}, dimensions={2}, use_global_device_ids=true | all-gather | bytes 435200 | tf_op jit(solution)/shard_map/all_gather | solution.py:83
  37.6 1.8 copy.49
  40.2 14.8 %all-gather.23.cloned.1.call-done = bf16[1,1280,480]{2,1,0:T(8,128)(2,1)} async-done(((bf16[1,80,480]{2,1,0:T(8,128)(2,1)}), bf16[1,1280,480]{2,1,0:T(8,128)(2,1)}) %all-gather.23.cloned.1.call-update) | async-done | bytes 1228816 | tf_op jit(solution)/shard_map/all_gather | solution.py:76
  55.0 30.0 %all-gather.13.cloned.1.call-done = bf16[1024,1280]{1,0:T(8,128)(2,1)} async-done(((bf16[128,1280]{1,0:T(8,128)(2,1)}), bf16[1024,1280]{1,0:T(8,128)(2,1)}) %all-gather.13.cloned.1.call-update) | async-done | bytes 2621456 | tf_op jit(solution)/shard_map/all_gather | solution.py:72
  85.1 3.6 convolution_convert_fusion.2
  88.6 3.7 fusion.112
  92.3 3.6 fusion.111
  95.9 3.2 fusion.31
  100.2 2.4 convolution_convert_fusion.1
  103.9 31.0 %reduce-scatter.3.cloned.1.call-done = bf16[128,1280]{1,0:T(8,128)(2,1)} async-done(((bf16[1024,1280]{1,0:T(8,128)(2,1)}), bf16[128,1280]{1,0:T(8,128)(2,1)}) %reduce-scatter.3.cloned.1.call-update) | async-done | bytes 327696 | tf_op jit(solution)/shard_map/reduce_scatter | solution.py:86
  137.5 43.5 %all-gather.25.cloned.1.call-done = bf16[1,1280,640]{2,1,0:T(8,128)(2,1)} async-done(((bf16[1,80,640]{2,1,0:T(8,128)(2,1)}), bf16[1,1280,640]{2,1,0:T(8,128)(2,1)}) %all-gather.25.cloned.1.call-update) | async-done | bytes 1638416 | tf_op jit(solution)/shard_map/all_gather | solution.py:97
  181.0 45.1 %all-gather.27.cloned.1.call-done = bf16[1,640,1280]{1,2,0:T(8,128)(2,1)} async-done(((bf16[1,640,80]{1,2,0:T(8,128)(2,1)}), bf16[1,640,1280]{1,2,0:T(8,128)(2,1)}) %all-gather.27.cloned.1.call-update) | async-done | bytes 1638416 | tf_op jit(solution)/shard_map/all_gather | solution.py:103
  226.1 29.3 %all-gather.15.cloned.1.call-done = bf16[1024,1280]{1,0:T(8,128)(2,1)} async-done(((bf16[128,1280]{1,0:T(8,128)(2,1)}), bf16[1024,1280]{1,0:T(8,128)(2,1)}) %all-gather.15.cloned.1.call-update) | async-done | bytes 2621456 | tf_op jit(solution)/shard_map/all_gather | solution.py:93
  255.3 13.0 %convolution_convert_fusion = bf16[1024,1280]{1,0:T(8,128)(2,1)} fusion(bf16[1,640,1280]{1,2,0:T(8,128)(2,1)} %all-gather.27.cloned.1.call-done, bf16[1024,1280]{1,0:T(8,128)(2,1)} %all-gather.15.cloned.1.call-done, bf16[1,1280,640]{2,1,0:T(8,128)(2,1)} %all-gather.25.cloned.1.call-done), kind=kOutput, calls=%fused_computation.12 | convolution fusion | flops 3399352320 | bytes 8519680 | tf_op jit(solution)/shard_map/dot_general | solution.py:101
  269.2 31.4 %reduce-scatter.5.cloned.1.call-done = bf16[128,1280]{1,0:T(8,128)(2,1)} async-done(((bf16[1024,1280]{1,0:T(8,128)(2,1)}), bf16[128,1280]{1,0:T(8,128)(2,1)}) %reduce-scatter.5.cloned.1.call-update) | async-done | bytes 327696 | tf_op jit(solution)/shard_map/reduce_scatter | solution.py:106
  305.1 55.3 %all-gather.19.cloned.1.call-done = bf16[5120,512]{1,0:T(8,128)(2,1)} async-done(((bf16[320,512]{1,0:T(8,128)(2,1)}), bf16[5120,512]{1,0:T(8,128)(2,1)}) %all-gather.19.cloned.1.call-update) | async-done | bytes 5242896 | tf_op jit(solution)/shard_map/all_gather | solution.py:117
  360.4 28.6 %all-gather.17.cloned.1.call-done = bf16[256,5120]{1,0:T(8,128)(2,1)} async-done(((bf16[32,5120]{1,0:T(8,128)(2,1)}), bf16[256,5120]{1,0:T(8,128)(2,1)}) %all-gather.17.cloned.1.call-update) | async-done | bytes 2621456 | tf_op jit(solution)/shard_map/all_gather | solution.py:112
  389.0 5.5 %convolution_convert_fusion.3 = bf16[256,512]{1,0:T(8,128)(2,1)} fusion(bf16[256,5120]{1,0:T(8,128)(2,1)} %all-gather.17.cloned.1.call-done, bf16[5120,512]{1,0:T(8,128)(2,1)} %all-gather.19.cloned.1.call-done), kind=kOutput, calls=%fused_computation.47 | convolution fusion | flops 1342308352 | bytes 8126464 | tf_op jit(solution)/shard_map/dot_general | solution.py:115
  397.0 48.9 %all-gather.21.cloned.1.call-done = bf16[4096,512]{1,0:T(8,128)(2,1)} async-done(((bf16[256,512]{1,0:T(8,128)(2,1)}), bf16[4096,512]{1,0:T(8,128)(2,1)}) %all-gather.21.cloned.1.call-update) | async-done | bytes 4194320 | tf_op jit(solution)/shard_map/all_gather | solution.py:134
  445.8 4.8 gather_fusion.2
  451.2 12.7 %psum.7 = f32[8]{0:T(128)S(1)} all-reduce(f32[8]{0:T(128)S(1)} %reduce_sum.118), channel_id=1, replica_groups=mesh['row'=16,'col'=8] {'col'}, use_global_device_ids=true, to_apply=%region_18.19 | all-reduce | flops 8 | bytes 64 | tf_op jit(solution)/shard_map/psum | solution.py:141
  464.3 15.0 %pmax.7 = f32[8]{0:T(128)} all-reduce(f32[8]{0:T(128)S(1)} %reduce_max.38), channel_id=1, replica_groups=mesh['row'=16,'col'=8] {'col'}, use_global_device_ids=true, to_apply=%region_21.22 | all-reduce | flops 8 | bytes 64 | tf_op jit(solution)/shard_map/pmax | solution.py:142
  (86 shorter events, 20.0 us)
Async XLA Ops:
  7.2 47.9 %all-gather.23.cloned.1.call-start = ((), (), s32[]{:S(2)}) async-start(), calls=%async_computation.9 | async-start | bytes 1392640 | tf_op jit(solution)/shard_map/all_gather | solution.py:76
  7.9 77.2 %all-gather.13.cloned.1.call-start = ((), (), s32[]{:S(2)}) async-start(), calls=%async_computation.2 | async-start | bytes 2949120 | tf_op jit(solution)/shard_map/all_gather | solution.py:72
  13.1 121.8 %reduce-scatter.3.cloned.1.call-start = ((), (), s32[]{:S(2)}) async-start(), calls=%async_computation.3 | async-start | bytes 2949120 | tf_op jit(solution)/shard_map/reduce_scatter | solution.py:86
  95.9 3.4 copy-start.6
  100.2 34.7 %copy-start = (bf16[128,1280]{1,0:T(8,128)(2,1)S(1)}, bf16[128,1280]{1,0:T(8,128)(2,1)}, u32[]{:S(2)}) copy-start(bf16[128,1280]{1,0:T(8,128)(2,1)} %param.12) | copy-start | bytes 983044
  102.7 78.3 %all-gather.25.cloned.1.call-start = ((), (), s32[]{:S(2)}) async-start(), calls=%async_computation.10 | async-start | bytes 1740800 | tf_op jit(solution)/shard_map/all_gather | solution.py:97
  103.3 122.8 %all-gather.27.cloned.1.call-start = ((), (), s32[]{:S(2)}) async-start(), calls=%async_computation.11 | async-start | bytes 1740800 | tf_op jit(solution)/shard_map/all_gather | solution.py:103
  103.8 151.5 %all-gather.15.cloned.1.call-start = ((), (), s32[]{:S(2)}) async-start(), calls=%async_computation.4 | async-start | bytes 2949120 | tf_op jit(solution)/shard_map/all_gather | solution.py:93
  137.3 163.3 %reduce-scatter.5.cloned.1.call-start = ((), (), s32[]{:S(2)}) async-start(), calls=%async_computation.5 | async-start | bytes 2949120 | tf_op jit(solution)/shard_map/reduce_scatter | solution.py:106
  268.3 34.6 %copy-start.2 = (f32[1280]{0:T(1024)S(1)}, f32[1280]{0:T(1024)}, u32[]{:S(2)}) copy-start(f32[1280]{0:T(1024)} %param.22) | copy-start | bytes 15364
  268.3 34.6 %copy-start.3 = (f32[1280]{0:T(1024)S(1)}, f32[1280]{0:T(1024)}, u32[]{:S(2)}) copy-start(f32[1280]{0:T(1024)} %param.21) | copy-start | bytes 15364
  268.4 92.0 %all-gather.19.cloned.1.call-start = ((), (), s32[]{:S(2)}) async-start(), calls=%async_computation.7 | async-start | bytes 5570560 | tf_op jit(solution)/shard_map/all_gather | solution.py:117
  269.1 119.9 %all-gather.17.cloned.1.call-start = ((), (), s32[]{:S(2)}) async-start(), calls=%async_computation.6 | async-start | bytes 2949120 | tf_op jit(solution)/shard_map/all_gather | solution.py:112
  305.1 89.5 %copy-start.1 = (s32[16,8]{0,1:T(8,128)S(1)}, s32[16,8]{0,1:T(8,128)}, u32[]{:S(2)}) copy-start(s32[16,8]{0,1:T(8,128)} %param.13) | copy-start | bytes 1540
  305.1 89.7 %copy-start.5 = (s32[128]{0:T(128)S(1)}, s32[128]{0:T(128)}, u32[]{:S(2)}) copy-start(s32[128]{0:T(128)} %param.14) | copy-start | bytes 1540
  305.1 140.7 %all-gather.21.cloned.1.call-start = ((), (), s32[]{:S(2)}) async-start(), calls=%async_computation.8 | async-start | bytes 4456448 | tf_op jit(solution)/shard_map/all_gather | solution.py:134
  464.0 16.3 %copy-start.4 = (f32[8]{0:T(128)}, f32[8]{0:T(128)S(1)}, u32[]{:S(2)}) copy-start(f32[8]{0:T(128)S(1)} %add_sqrt_fusion) | copy-start | bytes 100
Sparse Core Ops, SparseCore 0:
  10.1 44.8 all-gather.22
  57.3 27.7 all-gather.12
  102.8 32.0 reduce-scatter.2
  136.9 44.0 all-gather.24
  183.0 43.0 all-gather.26
  228.2 27.1 all-gather.14
  268.5 32.0 reduce-scatter.4
  302.7 57.6 all-gather.18
  362.7 26.2 all-gather.16
  394.7 51.1 all-gather.20
where the time goes:
time: 488 us; the launch traced here: 487 us
  waiting for transfers between devices  360 us (74%)
  blocking collectives  50.3 us (10%)
  matrix products  35.8 us (7%)
  between operations  14.4 us (3%)
  other arithmetic  13.2 us (3%)
  local copies, waits for them, and re-layouts  12.6 us (3%)
    all_gather x1, waiting for transfers between devices, local(): lax.all_gather(w_merge, 'row', axis=0, tiled=True)  55.3 us
    all_gather x1, waiting for transfers between devices, local(): piece = lax.all_gather(projected, 'row', axis=0, tiled=True)  48.9 us
    all_gather x1, waiting for transfers between devices, local(): lax.all_gather(w_down[0], 'row', axis=1, tiled=True)  45.1 us
    all_gather x1, waiting for transfers between devices, local(): lax.all_gather(w_up[0], 'row', axis=0, tiled=True)  43.5 us
    reduce_scatter x1, waiting for transfers between devices, local(): lax.psum_scatter(mlp_terms.astype(jnp.bfloat16), 'col', scatter_dimension...  31.4 us
    reduce_scatter x1, waiting for transfers between devices, local(): lax.psum_scatter(attn_terms.astype(jnp.bfloat16), 'col', scatter_dimensio...  31 us
    all_gather x1, waiting for transfers between devices, local(): normed_all = lax.all_gather(normed, 'col', axis=0, tiled=True)  30 us
    all_gather x1, waiting for transfers between devices, local(): normed_mlp = lax.all_gather(normed, 'col', axis=0, tiled=True)  29.3 us
  transfers between devices with their start and end apart: 10, of which 10 were waited for; matrix products, arithmetic and copies ran while one was open for 4% of the time, Pallas kernels for 0%

commit v1 on v0

--- a/solution.py
+++ b/solution.py
@@ -138,7 +138,11 @@
     blocks = placed.astype(jnp.float32).reshape(IMG_ROW, most, out_dev)
     squares = jnp.sum(blocks * blocks, axis=(1, 2))
     peaks = jnp.max(jnp.abs(blocks), axis=(1, 2))
-    squares = lax.psum(squares, "col")
+    size, result = (lax.axis_size("col"), squares)
+    for hop in [1 << k for k in range(size.bit_length() - 1)]:
+        route = [(i, i ^ hop) for i in range(size)]
+        result = result + lax.ppermute(result, "col", route)
+    squares = result
     peaks = lax.pmax(peaks, "col")
     slot_size = sizes_flat[request].astype(jnp.float32)
     req_norm = jnp.sqrt(squares / (slot_size * OUT) + 1e-06)

time: 488 us -> 484 us (level)
  blocking collectives: 50.3 us -> 34.9 us
  waiting for transfers between devices: 360 us -> 365 us
    psum x1 -> x0, blocking collectives: 12.7 us -> none  [local(): squares = lax.psum(squares, 'col')]
  transfers between devices with their start and end apart: 10 -> 13, of which waited for: 10 -> 12; matrix products, arithmetic and copies ran while one was open for 4% -> 4% of each run, Pallas kernels for 0% -> 0%
where the time goes in v1:
time: 484 us; the launch traced here: 479 us
  waiting for transfers between devices  365 us (75%)
  matrix products  35.8 us (7%)
  blocking collectives  34.9 us (7%)
  between operations  14.4 us (3%)
  other arithmetic  13.2 us (3%)
  local copies, waits for them, and re-layouts  12.6 us (3%)
    all_gather x1, waiting for transfers between devices, local(): lax.all_gather(w_merge, 'row', axis=0, tiled=True)  55.3 us
    all_gather x1, waiting for transfers between devices, local(): piece = lax.all_gather(projected, 'row', axis=0, tiled=True)  48.9 us
    all_gather x1, waiting for transfers between devices, local(): lax.all_gather(w_down[0], 'row', axis=1, tiled=True)  45.1 us
    all_gather x1, waiting for transfers between devices, local(): lax.all_gather(w_up[0], 'row', axis=0, tiled=True)  43.5 us
    reduce_scatter x1, waiting for transfers between devices, local(): lax.psum_scatter(mlp_terms.astype(jnp.bfloat16), 'col', scatter_dimension...  31.4 us
    reduce_scatter x1, waiting for transfers between devices, local(): lax.psum_scatter(attn_terms.astype(jnp.bfloat16), 'col', scatter_dimensio...  31 us
    all_gather x1, waiting for transfers between devices, local(): normed_all = lax.all_gather(normed, 'col', axis=0, tiled=True)  30 us
    all_gather x1, waiting for transfers between devices, local(): normed_mlp = lax.all_gather(normed, 'col', axis=0, tiled=True)  29.3 us
  transfers between devices with their start and end apart: 13, of which 12 were waited for; matrix products, arithmetic and copies ran while one was open for 4% of the time, Pallas kernels for 0%

profile of v1, /device:TPU:1, one launch (start us, length us, event | category | flops | bytes accessed | tf_op | source)
XLA Modules:
  0.0 479.2 jit_solution(11447357587388283016)
XLA Ops:
  11.1 2.0 fusion.48
  15.1 22.5 %all-gather.1 = bf16[1,160,1280]{1,0,2:T(2,128)(2,1)S(1)} all-gather(bf16[1,160,80]{1,0,2:T(2,128)(2,1)S(1)} %copy.48), channel_id=3, replica_groups=mesh['row'=16,'col'=8] {'row'}, dimensions={2}, use_global_device_ids=true | all-gather | bytes 435200 | tf_op jit(solution)/shard_map/all_gather | solution.py:83
  37.6 1.8 copy.49
  40.2 14.8 %all-gather.23.cloned.1.call-done = bf16[1,1280,480]{2,1,0:T(8,128)(2,1)} async-done(((bf16[1,80,480]{2,1,0:T(8,128)(2,1)}), bf16[1,1280,480]{2,1,0:T(8,128)(2,1)}) %all-gather.23.cloned.1.call-update) | async-done | bytes 1228816 | tf_op jit(solution)/shard_map/all_gather | solution.py:76
  55.0 30.0 %all-gather.13.cloned.1.call-done = bf16[1024,1280]{1,0:T(8,128)(2,1)} async-done(((bf16[128,1280]{1,0:T(8,128)(2,1)}), bf16[1024,1280]{1,0:T(8,128)(2,1)}) %all-gather.13.cloned.1.call-update) | async-done | bytes 2621456 | tf_op jit(solution)/shard_map/all_gather | solution.py:72
  85.1 3.6 convolution_convert_fusion.2
  88.6 3.7 fusion.112
  92.3 3.6 fusion.111
  95.9 3.2 fusion.31
  100.2 2.4 convolution_convert_fusion.1
  103.9 31.0 %reduce-scatter.3.cloned.1.call-done = bf16[128,1280]{1,0:T(8,128)(2,1)} async-done(((bf16[1024,1280]{1,0:T(8,128)(2,1)}), bf16[128,1280]{1,0:T(8,128)(2,1)}) %reduce-scatter.3.cloned.1.call-update) | async-done | bytes 327696 | tf_op jit(solution)/shard_map/reduce_scatter | solution.py:86
  137.5 43.5 %all-gather.25.cloned.1.call-done = bf16[1,1280,640]{2,1,0:T(8,128)(2,1)} async-done(((bf16[1,80,640]{2,1,0:T(8,128)(2,1)}), bf16[1,1280,640]{2,1,0:T(8,128)(2,1)}) %all-gather.25.cloned.1.call-update) | async-done | bytes 1638416 | tf_op jit(solution)/shard_map/all_gather | solution.py:97
  181.0 45.1 %all-gather.27.cloned.1.call-done = bf16[1,640,1280]{1,2,0:T(8,128)(2,1)} async-done(((bf16[1,640,80]{1,2,0:T(8,128)(2,1)}), bf16[1,640,1280]{1,2,0:T(8,128)(2,1)}) %all-gather.27.cloned.1.call-update) | async-done | bytes 1638416 | tf_op jit(solution)/shard_map/all_gather | solution.py:103
  226.1 29.3 %all-gather.15.cloned.1.call-done = bf16[1024,1280]{1,0:T(8,128)(2,1)} async-done(((bf16[128,1280]{1,0:T(8,128)(2,1)}), bf16[1024,1280]{1,0:T(8,128)(2,1)}) %all-gather.15.cloned.1.call-update) | async-done | bytes 2621456 | tf_op jit(solution)/shard_map/all_gather | solution.py:93
  255.3 13.0 %convolution_convert_fusion = bf16[1024,1280]{1,0:T(8,128)(2,1)} fusion(bf16[1,640,1280]{1,2,0:T(8,128)(2,1)} %all-gather.27.cloned.1.call-done, bf16[1024,1280]{1,0:T(8,128)(2,1)} %all-gather.15.cloned.1.call-done, bf16[1,1280,640]{2,1,0:T(8,128)(2,1)} %all-gather.25.cloned.1.call-done), kind=kOutput, calls=%fused_computation.12 | convolution fusion | flops 3399352320 | bytes 8519680 | tf_op jit(solution)/shard_map/dot_general | solution.py:101
  269.2 31.4 %reduce-scatter.5.cloned.1.call-done = bf16[128,1280]{1,0:T(8,128)(2,1)} async-done(((bf16[1024,1280]{1,0:T(8,128)(2,1)}), bf16[128,1280]{1,0:T(8,128)(2,1)}) %reduce-scatter.5.cloned.1.call-update) | async-done | bytes 327696 | tf_op jit(solution)/shard_map/reduce_scatter | solution.py:106
  305.1 55.3 %all-gather.19.cloned.1.call-done = bf16[5120,512]{1,0:T(8,128)(2,1)} async-done(((bf16[320,512]{1,0:T(8,128)(2,1)}), bf16[5120,512]{1,0:T(8,128)(2,1)}) %all-gather.19.cloned.1.call-update) | async-done | bytes 5242896 | tf_op jit(solution)/shard_map/all_gather | solution.py:117
  360.4 28.6 %all-gather.17.cloned.1.call-done = bf16[256,5120]{1,0:T(8,128)(2,1)} async-done(((bf16[32,5120]{1,0:T(8,128)(2,1)}), bf16[256,5120]{1,0:T(8,128)(2,1)}) %all-gather.17.cloned.1.call-update) | async-done | bytes 2621456 | tf_op jit(solution)/shard_map/all_gather | solution.py:112
  389.0 5.5 %convolution_convert_fusion.3 = bf16[256,512]{1,0:T(8,128)(2,1)} fusion(bf16[256,5120]{1,0:T(8,128)(2,1)} %all-gather.17.cloned.1.call-done, bf16[5120,512]{1,0:T(8,128)(2,1)} %all-gather.19.cloned.1.call-done), kind=kOutput, calls=%fused_computation.47 | convolution fusion | flops 1342308352 | bytes 8126464 | tf_op jit(solution)/shard_map/dot_general | solution.py:115
  397.0 48.9 %all-gather.21.cloned.1.call-done = bf16[4096,512]{1,0:T(8,128)(2,1)} async-done(((bf16[256,512]{1,0:T(8,128)(2,1)}), bf16[4096,512]{1,0:T(8,128)(2,1)}) %all-gather.21.cloned.1.call-update) | async-done | bytes 4194320 | tf_op jit(solution)/shard_map/all_gather | solution.py:134
  445.8 4.8 %gather_fusion.2 = bf16[384,512]{1,0:T(8,128)(2,1)S(1)} fusion(bf16[4096,512]{1,0:T(8,128)(2,1)} %all-gather.21.cloned.1.call-done, s32[1024]{0:T(1024)S(1)} %pad_clamp_fusion), kind=kCustom, calls=%fused_computation.2 | custom fusion | bytes 787968 | tf_op jit(solution)/shard_map/jit(_take)/gather | solution.py:136
  452.3 12.4 %pmax.7 = f32[8]{0:T(128)} all-reduce(f32[8]{0:T(128)S(1)} %reduce_max.38), channel_id=1, replica_groups=mesh['row'=16,'col'=8] {'col'}, use_global_device_ids=true, to_apply=%region_20.21 | all-reduce | flops 8 | bytes 64 | tf_op jit(solution)/shard_map/pmax | solution.py:146
  464.8 2.6 collective-permute-done.1
  467.3 2.2 collective-permute-start.2
  (93 shorter events, 23.9 us)
Async XLA Ops:
  7.2 47.9 %all-gather.23.cloned.1.call-start = ((), (), s32[]{:S(2)}) async-start(), calls=%async_computation.9 | async-start | bytes 1392640 | tf_op jit(solution)/shard_map/all_gather | solution.py:76
  7.9 77.2 %all-gather.13.cloned.1.call-start = ((), (), s32[]{:S(2)}) async-start(), calls=%async_computation.2 | async-start | bytes 2949120 | tf_op jit(solution)/shard_map/all_gather | solution.py:72
  13.1 121.8 %reduce-scatter.3.cloned.1.call-start = ((), (), s32[]{:S(2)}) async-start(), calls=%async_computation.3 | async-start | bytes 2949120 | tf_op jit(solution)/shard_map/reduce_scatter | solution.py:86
  95.9 3.4 copy-start.6
  100.2 34.7 %copy-start = (bf16[128,1280]{1,0:T(8,128)(2,1)S(1)}, bf16[128,1280]{1,0:T(8,128)(2,1)}, u32[]{:S(2)}) copy-start(bf16[128,1280]{1,0:T(8,128)(2,1)} %param.12) | copy-start | bytes 983044
  102.7 78.3 %all-gather.25.cloned.1.call-start = ((), (), s32[]{:S(2)}) async-start(), calls=%async_computation.10 | async-start | bytes 1740800 | tf_op jit(solution)/shard_map/all_gather | solution.py:97
  103.3 122.8 %all-gather.27.cloned.1.call-start = ((), (), s32[]{:S(2)}) async-start(), calls=%async_computation.11 | async-start | bytes 1740800 | tf_op jit(solution)/shard_map/all_gather | solution.py:103
  103.8 151.5 %all-gather.15.cloned.1.call-start = ((), (), s32[]{:S(2)}) async-start(), calls=%async_computation.4 | async-start | bytes 2949120 | tf_op jit(solution)/shard_map/all_gather | solution.py:93
  137.3 163.3 %reduce-scatter.5.cloned.1.call-start = ((), (), s32[]{:S(2)}) async-start(), calls=%async_computation.5 | async-start | bytes 2949120 | tf_op jit(solution)/shard_map/reduce_scatter | solution.py:106
  268.3 34.6 %copy-start.2 = (f32[1280]{0:T(1024)S(1)}, f32[1280]{0:T(1024)}, u32[]{:S(2)}) copy-start(f32[1280]{0:T(1024)} %param.22) | copy-start | bytes 15364
  268.3 34.6 %copy-start.3 = (f32[1280]{0:T(1024)S(1)}, f32[1280]{0:T(1024)}, u32[]{:S(2)}) copy-start(f32[1280]{0:T(1024)} %param.21) | copy-start | bytes 15364
  268.4 92.0 %all-gather.19.cloned.1.call-start = ((), (), s32[]{:S(2)}) async-start(), calls=%async_computation.7 | async-start | bytes 5570560 | tf_op jit(solution)/shard_map/all_gather | solution.py:117
  269.1 119.9 %all-gather.17.cloned.1.call-start = ((), (), s32[]{:S(2)}) async-start(), calls=%async_computation.6 | async-start | bytes 2949120 | tf_op jit(solution)/shard_map/all_gather | solution.py:112
  305.1 89.5 %copy-start.1 = (s32[16,8]{0,1:T(8,128)S(1)}, s32[16,8]{0,1:T(8,128)}, u32[]{:S(2)}) copy-start(s32[16,8]{0,1:T(8,128)} %param.13) | copy-start | bytes 1540
  305.1 89.7 %copy-start.5 = (s32[128]{0:T(128)S(1)}, s32[128]{0:T(128)}, u32[]{:S(2)}) copy-start(s32[128]{0:T(128)} %param.14) | copy-start | bytes 1540
  305.1 140.7 %all-gather.21.cloned.1.call-start = ((), (), s32[]{:S(2)}) async-start(), calls=%async_computation.8 | async-start | bytes 4456448 | tf_op jit(solution)/shard_map/all_gather | solution.py:134
  451.4 13.3 %collective-permute-start = (f32[8]{0:T(128)S(1)}, f32[8]{0:T(128)S(1)}, u32[]{:S(2)}, u32[]{:S(2)}) collective-permute-start(f32[8]{0:T(128)S(1)} %reduce_sum.118), channel_id=1, source_target_pairs={{0,1},{1,0},{2,3},{3,2},{4,5},{5,4},{6,7},{7,6},{8,9},{9,8},{10,11... | collective-permute-start | bytes 104 | tf_op jit(solution)/shard_map/ppermute | solution.py:144
  464.7 2.6 collective-permute-start.1
  467.3 3.9 collective-permute-start.2
  471.3 1.1 copy-start.4
Sparse Core Ops, SparseCore 0:
  10.1 44.8 all-gather.22
  57.3 27.7 all-gather.12
  102.8 32.0 reduce-scatter.2
  136.9 44.0 all-gather.24
  183.0 43.0 all-gather.26
  228.2 27.1 all-gather.14
  268.5 32.0 reduce-scatter.4
  302.7 57.6 all-gather.18
  362.7 26.2 all-gather.16
  394.7 51.1 all-gather.20
